TPU v7x, 256 devices: a whole 4x4x8 slice. The times are simulated.
256 devices in a mesh: box: 64 (over x, z, core), blk: 4 (over y).
Axes of the slice: x: 4, y: 4, z: 8, core: 2. Of those that a mesh axis runs over, the one named last changes fastest.
Arguments:
- operator_map: float32 [64, 1536, 1536], P('box', 'blk'), may hold values from -0.5 to 2, as said below
- face_list: int32 [64, 256], replicated, may hold values from 0 to 1535, as said below
Outputs:
- merged: float32 [64, 1536, 3072], P('box', 'blk')
Inputs may be any that keep to these rules, and one draw needn't show every extreme that they name: `operator_map`: each box's map is symmetric; its diagonal lies in 1 to 2. Points 6 i + f and 6 j + f with the same f lie on one face: their entry is zero unless |i - j| is 1 or 2, and then lies in -0.245 to -0.12. Entries between points of different faces lie in -0.5 to 0.5. `face_list`: entry i of box b's list is 6 i + f_b with f_b from 0 to 5, so each list rises; boxes 2p and 2p + 1 list opposite faces, f = 2 a + 1 and f = 2 a, with one a from 0 to 2 for each pair, entry i of one facing entry i of the other.
All inputs are finite; a program needn't handle non-finite values.
Results may differ from a plain program's by a relative error of at most 0.0003.
Values sent between devices are 32-bit elements; how exact they have to be, the bound alone decides.
A program may use at most 64 MiB of HBM per device.

v0:
```python
import jax
import jax.numpy as jnp
from jax import lax
from jax.sharding import PartitionSpec as P


def from_partner(block, axis, apart):
    count = lax.axis_size(axis)
    route = []
    for low in range(count):
        high = low | 1 << apart
        if high != low and high < count:
            route += [(low, high), (high, low)]
    return lax.ppermute(block, axis, route)


def on_device(operator_map, face_list):
    blocks = lax.axis_size("blk")
    box_index = lax.axis_index("box")
    blk_index = lax.axis_index("blk")
    local_rows = operator_map[0]
    row_count = local_rows.shape[0]
    face_size = face_list.shape[1]
    per_block = face_size // blocks
    own_list = lax.dynamic_index_in_dim(face_list, box_index, 0, keepdims=False)
    sibling_index = jnp.bitwise_xor(box_index, 1)
    sibling_list = lax.dynamic_index_in_dim(face_list, sibling_index, 0, keepdims=False)
    local_list = (
        lax.dynamic_slice_in_dim(own_list, blk_index * per_block, per_block) - blk_index * row_count
    )
    picked = jnp.take(local_rows, local_list, axis=0)
    face_block = lax.all_gather(picked, "blk", axis=0, tiled=True)
    own_face = jnp.take(face_block, own_list, axis=1)
    is_lower = jnp.bitwise_and(box_index, 1) == 0
    coupling = jnp.take(local_rows, own_list, axis=1)
    sibling_block = from_partner(face_block, "box", 0)
    schur_sum = own_face + jnp.take(sibling_block, sibling_list, axis=1)
    factor = jnp.linalg.cholesky(schur_sum)
    lower_part = jnp.where(is_lower, face_block, sibling_block)
    upper_part = jnp.where(is_lower, sibling_block, face_block)
    weights = jax.scipy.linalg.cho_solve((factor, True), coupling.T).T
    correction = jnp.dot(
        weights,
        jnp.concatenate([lower_part, upper_part], axis=1),
        precision=lax.Precision.HIGHEST,
        preferred_element_type=jnp.float32,
    )
    blank_rows = jnp.zeros_like(local_rows)
    diagonal_part = jnp.concatenate(
        [jnp.where(is_lower, local_rows, blank_rows), jnp.where(is_lower, blank_rows, local_rows)],
        axis=1,
    )
    return (diagonal_part - correction)[None, :, :]


def solution(mesh):
    in_specs = (P("box", "blk", None), P())
    out_specs = P("box", "blk", None)
    return jax.shard_map(
        on_device, mesh=mesh, in_specs=in_specs, out_specs=out_specs, check_vma=False
    )
```

profile of v0, /device:TPU:1, one launch (start us, length us, event | category | flops | bytes accessed | tf_op | source)
XLA Modules:
  0.0 132.3 jit_solution(14960521785130965118)
XLA Ops:
  6.5 0.8 compare_and_fusion.2
  7.3 2.7 %gather_fusion = f32[64,1536]{1,0:T(8,128)S(1)} fusion(f32[384,1536]{1,0:T(8,128)} %bitcast.56, s32[1024]{0:T(1024)S(1)} %pad_clamp_fusion.3), kind=kCustom, calls=%fused_computation.2 | custom fusion | bytes 786688 | tf_op jit(solution)/shard_map/jit(_take)/gather | solution.py:31
  10.1 0.9 broadcast_select_fusion.5
  11.0 2.0 %copy.10 = f32[384,1536]{0,1:T(8,128)} copy(f32[384,1536]{1,0:T(8,128)S(1)} %bitcast.57) | data formatting | bytes 4718592 | tf_op jit(solution)/shard_map/squeeze | solution.py:21
  12.9 0.7 compare_select_fusion
  13.6 2.8 %gather_fusion.1 = f32[256,384]{1,0:T(8,128)S(1)} fusion(f32[384,1536]{0,1:T(8,128)} %copy.10, s32[1024]{0:T(1024)S(1)} %pad_clamp_fusion), kind=kCustom, calls=%fused_computation.3 | custom fusion | bytes 787456 | tf_op jit(solution)/shard_map/jit(_take)/gather | solution.py:35
  16.4 0.7 constant_dynamic-slice_fusion.1
  17.2 26.8 %all-gather.2.cloned.1.call-done = f32[256,1536]{1,0:T(8,128)} async-done(((f32[64,1536]{1,0:T(8,128)}), f32[256,1536]{1,0:T(8,128)}) %all-gather.2.cloned.1.call-update) | async-done | bytes 1572880 | tf_op jit(solution)/shard_map/all_gather | solution.py:32
  44.0 0.7 collective-permute-start
  44.8 2.9 %broadcast_select_fusion.1 = (f32[384,1536]{1,0:T(8,128)}, f32[384,1536]{1,0:T(8,128)}) fusion(pred[]{:T(512)S(6)} %eq.3, f32[1,384,1536]{2,1,0:T(8,128)S(1)} %copy-done), kind=kLoop, calls=%fused_computation.12 | loop fusion | flops 1179648 | bytes 7077889 | tf_op jit(solution)/shard_map/jit(_where)/select_n | solution.py:50
  47.7 1.9 %copy.7 = f32[256,1536]{0,1:T(8,128)S(1)} copy(f32[256,1536]{1,0:T(8,128)} %all-gather.2.cloned.1.call-done) | data formatting | bytes 3145728 | tf_op jit(solution)/shard_map/all_gather | solution.py:32
  49.6 1.0 gather_fusion.2
  50.5 1.9 %copy.8 = f32[256,1536]{0,1:T(8,128)S(1)} copy(f32[256,1536]{1,0:T(8,128)} %collective-permute-done) | data formatting | bytes 3145728 | tf_op jit(solution)/shard_map/ppermute | solution.py:14
  52.4 1.0 gather_fusion.3
  53.7 11.7 %cholesky.50 = f32[128,128]{1,0:T(8,128)S(1)} custom-call(f32[128,128]{1,0:T(8,128)S(1)} %cholesky.118), custom_call_target="Cholesky" | custom-call | tf_op jit(solution)/shard_map/jit(cholesky)/cholesky | solution.py:38
  65.5 0.7 compare_reduce_fusion.1
  66.2 9.8 %custom-call.18 = f32[1,128,128]{1,2,0:T(8,128)S(1)} custom-call(f32[1,128,128]{2,1,0:T(8,128)S(1)} %get-tuple-element.35), custom_call_target="InvertDiagBlocksLowerTriangular" | custom-call | tf_op jit(solution)/shard_map/jit(cholesky)/cholesky | solution.py:38
  76.5 11.9 %cholesky.105 = f32[128,128]{1,0:T(8,128)S(1)} custom-call(f32[128,128]{1,0:T(8,128)S(1)} %convolution_subtract_fusion.2), custom_call_target="Cholesky" | custom-call | tf_op jit(solution)/shard_map/jit(cholesky)/cholesky | solution.py:38
  88.4 0.6 compare_reduce_fusion
  90.4 4.1 %while.1 = (s32[]{:T(128)}, f32[256,256]{1,0:T(8,128)S(1)}, s32[2,2]{1,0:T(2,128)S(1)}, f32[2,128,128]{2,1,0:T(8,128)S(1)}, s32[]{:T(128)}) while((s32[]{:T(128)}, f32[256,256]{1,0:T(8,128)S(1)}, s32[2,2]{1,0:T(2,128)S(1)}, f32[2,128,128]{2,1,0:T(8,128)S(1)}, s32[]{:T(128)}) %tuple.28), condition=%wide.while_cond, body=%wide.while_body.sunk | while | flops 2 | bytes 131189 | solution.py:41
  90.4 0.7 fusion.29
  91.1 1.3 %bitcast_dynamic-update-slice_fusion.2 = f32[2,128,128]{2,1,0:T(8,128)S(1)} fusion(f32[2,128,128]{2,1,0:T(8,128)S(1)} %get-tuple-element.77, s32[]{:T(128)S(6)} %copy.16, f32[256,256]{1,0:T(8,128)S(1)} %get-tuple-element.80, s32[]{:T(128)} %bitcast.54, s32[]{:T(128)} %bitcast.55), kind=kLoop, calls=%fused_computation.4.clone.1 | loop fusion | bytes 131084 | tf_op jit(solution)/shard_map/jit(_cho_solve)/triangular_solve
  92.5 0.7 fusion.29
  93.1 1.3 %bitcast_dynamic-update-slice_fusion.2 = f32[2,128,128]{2,1,0:T(8,128)S(1)} fusion(f32[2,128,128]{2,1,0:T(8,128)S(1)} %get-tuple-element.77, s32[]{:T(128)S(6)} %copy.16, f32[256,256]{1,0:T(8,128)S(1)} %get-tuple-element.80, s32[]{:T(128)} %bitcast.54, s32[]{:T(128)} %bitcast.55), kind=kLoop, calls=%fused_computation.4.clone.1 | loop fusion | bytes 131084 | tf_op jit(solution)/shard_map/jit(_cho_solve)/triangular_solve
  94.5 19.7 %custom-call.19 = f32[2,128,128]{1,2,0:T(8,128)S(1)} custom-call(f32[2,128,128]{2,1,0:T(8,128)S(1)} %get-tuple-element.13), custom_call_target="InvertDiagBlocksLowerTriangular" | custom-call | tf_op jit(solution)/shard_map/jit(_cho_solve)/triangular_solve | solution.py:41
  114.2 0.4 fusion.8
  114.5 0.3 convolution_subtract_fusion.1
  114.9 0.4 fusion.15
  115.6 0.4 convolution_subtract_fusion
  116.3 1.8 %broadcast_select_fusion.3 = (f32[256,1536]{1,0:T(8,128)S(1)}, f32[256,1536]{1,0:T(8,128)S(1)}) fusion(f32[256,1536]{1,0:T(8,128)S(1)} %copy-done.3, f32[256,1536]{1,0:T(8,128)} %collective-permute-done, pred[]{:T(512)S(6)} %eq.3), kind=kLoop, calls=%fused_computation.17 | loop fusion | flops 786432 | bytes 6291457 | tf_op jit(solution)/shard_map/jit(_where)/select_n | solution.py:39
  118.4 0.7 copy-done.2
  119.1 6.4 %fusion = f32[1,384,3072]{2,1,0:T(8,128)} fusion(f32[384,1536]{1,0:T(8,128)S(1)} %copy-done.2, f32[384,1536]{1,0:T(8,128)S(1)} %copy-done.1, f32[256,1536]{1,0:T(8,128)S(1)} %get-tuple-element.29, f32[256,1536]{1,0:T(8,128)S(1)} %get-tuple-element.28, f32[128,384]{1,0:T(8,128)S(1)} %fusion.14, f32[128,384]{1,0:T(8,128)S(1)} %fusion.13), kind=kOutput, calls=%fused_computation.7 | convolution fusion | flops 3627122688 | bytes 12976128 | tf_op jit(solution)/shard_map/dot_general | solution.py:42
  (36 shorter events, 2.1 us)
Async XLA Ops:
  6.5 37.5 %all-gather.2.cloned.1.call-start = ((), (), s32[]{:S(2)}) async-start(), calls=%async_computation | async-start | bytes 1966080 | tf_op jit(solution)/shard_map/all_gather | solution.py:32
  7.3 3.6 %copy-start = (f32[1,384,1536]{2,1,0:T(8,128)S(1)}, f32[1,384,1536]{2,1,0:T(8,128)}, u32[]{:S(2)}) copy-start(f32[1,384,1536]{2,1,0:T(8,128)} %param.4) | copy-start | bytes 7077892
  44.0 6.5 %collective-permute-start = (f32[256,1536]{1,0:T(8,128)}, f32[256,1536]{1,0:T(8,128)}, u32[]{:S(2)}, u32[]{:S(2)}) collective-permute-start(f32[256,1536]{1,0:T(8,128)} %all-gather.2.cloned.1.call-done), channel_id=1, source_target_pairs={{0,4},{4,0},{8,12},{12,8},{16,20},{20,16},{24,28},{28,24},{32,36},... | collective-permute-start | bytes 4718600 | tf_op jit(solution)/shard_map/ppermute | solution.py:14
  76.5 39.7 %copy-start.3 = (f32[256,1536]{1,0:T(8,128)S(1)}, f32[256,1536]{1,0:T(8,128)}, u32[]{:S(2)}) copy-start(f32[256,1536]{1,0:T(8,128)} %all-gather.2.cloned.1.call-done) | copy-start | bytes 4718596
  116.3 2.1 %copy-start.1 = (f32[384,1536]{1,0:T(8,128)S(1)}, f32[384,1536]{1,0:T(8,128)}, u32[]{:S(2)}) copy-start(f32[384,1536]{1,0:T(8,128)} %get-tuple-element.30) | copy-start | bytes 7077892
  116.3 2.8 %copy-start.2 = (f32[384,1536]{1,0:T(8,128)S(1)}, f32[384,1536]{1,0:T(8,128)}, u32[]{:S(2)}) copy-start(f32[384,1536]{1,0:T(8,128)} %get-tuple-element.31) | copy-start | bytes 7077892
Sparse Core Ops, SparseCore 0:
  11.1 32.8 all-gather.1
where the time goes:
time: 133 us; the launch traced here: 132 us
  other arithmetic  61.8 us (46%)
  waiting for transfers between devices  26.9 us (20%)
  local copies, waits for them, and re-layouts  19.1 us (14%)
  between operations  14.9 us (11%)
  matrix products  8.89 us (7%)
    another operation x7, other arithmetic, on_device(): factor = jnp.linalg.cholesky(schur_sum)  34.8 us
    all_gather x1, waiting for transfers between devices, on_device(): face_block = lax.all_gather(picked, 'blk', axis=0, tiled=True)  26.8 us
    another operation x3, other arithmetic, on_device(): weights = jax.scipy.linalg.cho_solve((factor, True), coupling.T).T  19.7 us
    dot_general x1, matrix products, on_device(): jnp.dot(weights, jnp.concatenate([lower_part, upper_part], axis=1), preci...  6.37 us
    another operation x6, local copies, waits for them, and re-layouts  4.03 us
    select_n x1, other arithmetic, on_device(): jnp.where(is_lower, local_rows, blank_rows)  2.87 us
    gather x1, local copies, waits for them, and re-layouts, on_device(): coupling = jnp.take(local_rows, own_list, axis=1)  2.8 us
    gather x1, local copies, waits for them, and re-layouts, on_device(): picked = jnp.take(local_rows, local_list, axis=0)  2.71 us
  transfers between devices with their start and end apart: 2, of which 1 were waited for; matrix products, arithmetic and copies ran while one was open for 9% of the time, Pallas kernels for 0%

commit v1 on v0

--- a/solution.py
+++ b/solution.py
@@ -29,7 +29,9 @@
         lax.dynamic_slice_in_dim(own_list, blk_index * per_block, per_block) - blk_index * row_count
     )
     picked = jnp.take(local_rows, local_list, axis=0)
-    face_block = lax.all_gather(picked, "blk", axis=0, tiled=True)
+    face_block = jnp.concatenate(
+        lax.all_to_all(jnp.stack([picked] * lax.axis_size("blk")), "blk", 0, 0), axis=0
+    )
     own_face = jnp.take(face_block, own_list, axis=1)
     is_lower = jnp.bitwise_and(box_index, 1) == 0
     coupling = jnp.take(local_rows, own_list, axis=1)

time: 133 us -> 119 us (0.89)
  waiting for transfers between devices: 26.9 us -> 12.3 us
  between operations: 14.9 us -> 1.54 us
  starting transfers between devices: 0.68 us -> 8.39 us
  matrix products: 8.89 us -> 12.4 us
  local copies, waits for them, and re-layouts: 19.1 us -> 22.4 us
    all_gather x1 -> x0, waiting for transfers between devices: 26.8 us -> none  [on_device(): face_block = lax.all_gather(picked, 'blk', axis=0, tiled=True)]
    all_to_all x0 -> x1, waiting for transfers between devices: none -> 12.3 us  [on_device(): lax.all_to_all(jnp.stack([picked] * lax.axis_size('blk')), 'blk', 0, 0)]
    all_to_all x0 -> x1, starting transfers between devices: none -> 5 us  [on_device(): lax.all_to_all(jnp.stack([picked] * lax.axis_size('blk')), 'blk', 0, 0)]
    dot_general x1, matrix products: 6.37 us -> 9.86 us  [on_device(): jnp.dot(weights, jnp.concatenate([lower_part, upper_part], axis=1), preci...]
    reshape x0 -> x1, local copies, waits for them, and re-layouts: none -> 3.01 us  [on_device(): jnp.concatenate(lax.all_to_all(jnp.stack([picked] * lax.axis_size('blk'))...]
    ppermute x1, starting transfers between devices: 0.68 us -> 3.38 us  [from_partner(): return lax.ppermute(block, axis, route)]
    ppermute x1 -> x0, local copies, waits for them, and re-layouts: 1.87 us -> none  [from_partner(): return lax.ppermute(block, axis, route)]
    all_gather x1 -> x0, local copies, waits for them, and re-layouts: 1.87 us -> none  [on_device(): face_block = lax.all_gather(picked, 'blk', axis=0, tiled=True)]
  transfers between devices with their start and end apart: 2 -> 2, of which waited for: 1 -> 1; matrix products, arithmetic and copies ran while one was open for 9% -> 10% of each run, Pallas kernels for 0% -> 0%
where the time goes in v1:
time: 119 us; the launch traced here: 118 us
  other arithmetic  60.9 us (51%)
  local copies, waits for them, and re-layouts  22.4 us (19%)
  matrix products  12.4 us (10%)
  waiting for transfers between devices  12.3 us (10%)
  starting transfers between devices  8.39 us (7%)
  between operations  1.54 us (1%)
    another operation x7, other arithmetic, on_device(): factor = jnp.linalg.cholesky(schur_sum)  34.7 us
    another operation x3, other arithmetic, on_device(): weights = jax.scipy.linalg.cho_solve((factor, True), coupling.T).T  19.7 us
    all_to_all x1, waiting for transfers between devices, on_device(): lax.all_to_all(jnp.stack([picked] * lax.axis_size('blk')), 'blk', 0, 0)  12.3 us
    dot_general x1, matrix products, on_device(): jnp.dot(weights, jnp.concatenate([lower_part, upper_part], axis=1), preci...  9.86 us
    all_to_all x1, starting transfers between devices, on_device(): lax.all_to_all(jnp.stack([picked] * lax.axis_size('blk')), 'blk', 0, 0)  5 us
    another operation x6, local copies, waits for them, and re-layouts  3.99 us
    ppermute x1, starting transfers between devices, from_partner(): return lax.ppermute(block, axis, route)  3.38 us
    reshape x1, local copies, waits for them, and re-layouts, on_device(): jnp.concatenate(lax.all_to_all(jnp.stack([picked] * lax.axis_size('blk'))...  3.01 us
  transfers between devices with their start and end apart: 2, of which 1 were waited for; matrix products, arithmetic and copies ran while one was open for 10% of the time, Pallas kernels for 0%

profile of v1, /device:TPU:1, one launch (start us, length us, event | category | flops | bytes accessed | tf_op | source)
XLA Modules:
  0.0 118.1 jit_solution(4244030206186329736)
XLA Ops:
  0.0 0.8 compare_and_fusion.2
  0.8 2.6 %gather_fusion = f32[64,1536]{1,0:T(8,128)S(1)} fusion(f32[384,1536]{1,0:T(8,128)} %bitcast.57, s32[1024]{0:T(1024)S(1)} %pad_clamp_fusion.3), kind=kCustom, calls=%fused_computation.2 | custom fusion | bytes 786688 | tf_op jit(solution)/shard_map/jit(_take)/gather | solution.py:31
  3.5 1.3 %stack.2 = f32[4,64,1536]{2,1,0:T(8,128)} broadcast(f32[64,1536]{1,0:T(8,128)S(1)} %broadcast_select_fusion.5), dimensions={1,2} | broadcast | bytes 1966080 | tf_op jit(solution)/shard_map/stack | solution.py:33
  4.8 5.0 %all-to-all-start = ((f32[4,64,1536]{2,1,0:T(8,128)}), f32[4,64,1536]{2,1,0:T(8,128)}, u32[]{:S(2)}, u32[]{:S(2)}) async-start(f32[4,64,1536]{2,1,0:T(8,128)} %stack.2), calls=%async_computation | async-start | bytes 3145728 | tf_op jit(solution)/shard_map/all_to_all | solution.py:33
  9.8 1.9 %copy.9 = f32[384,1536]{0,1:T(8,128)} copy(f32[384,1536]{1,0:T(8,128)S(1)} %bitcast.58) | data formatting | bytes 4718592 | tf_op jit(solution)/shard_map/squeeze | solution.py:21
  11.8 0.7 compare_select_fusion
  12.5 2.8 %gather_fusion.1 = f32[256,384]{1,0:T(8,128)S(1)} fusion(f32[384,1536]{0,1:T(8,128)} %copy.9, s32[1024]{0:T(1024)S(1)} %pad_clamp_fusion), kind=kCustom, calls=%fused_computation.3 | custom fusion | bytes 787456 | tf_op jit(solution)/shard_map/jit(_take)/gather | solution.py:37
  15.3 0.7 constant_dynamic-slice_fusion.1
  16.0 12.3 %all-to-all-done = f32[4,64,1536]{2,1,0:T(8,128)} async-done(((f32[4,64,1536]{2,1,0:T(8,128)}), f32[4,64,1536]{2,1,0:T(8,128)}, u32[]{:S(2)}, u32[]{:S(2)}) %all-to-all-start) | async-done | bytes 1572896 | tf_op jit(solution)/shard_map/all_to_all | solution.py:33
  28.3 3.0 %copy.6 = f32[256,1536]{0,1:T(8,128)} copy(f32[256,1536]{1,0:T(8,128)} %bitcast.5) | data formatting | bytes 3145728 | tf_op jit(solution)/shard_map/reshape | solution.py:32
  31.3 3.4 %collective-permute-start = (f32[256,1536]{0,1:T(8,128)}, f32[256,1536]{0,1:T(8,128)}, u32[]{:S(2)}, u32[]{:S(2)}) collective-permute-start(f32[256,1536]{0,1:T(8,128)} %copy.6), channel_id=1, source_target_pairs={{0,4},{4,0},{8,12},{12,8},{16,20},{20,16},{24,28},{28,24},{32,36},... | collective-permute-start | bytes 4718600 | tf_op jit(solution)/shard_map/ppermute | solution.py:14
  34.8 2.9 %broadcast_select_fusion.1 = (f32[384,1536]{1,0:T(8,128)}, f32[384,1536]{1,0:T(8,128)}) fusion(pred[]{:T(512)S(6)} %eq.3, f32[1,384,1536]{2,1,0:T(8,128)S(1)} %copy-done), kind=kLoop, calls=%fused_computation.12 | loop fusion | flops 1179648 | bytes 7077889 | tf_op jit(solution)/shard_map/jit(_where)/select_n | solution.py:52
  37.7 2.4 %gather_fusion.2 = f32[256,256]{1,0:T(8,128)S(1)} fusion(f32[256,1536]{0,1:T(8,128)} %copy.6, s32[1024]{0:T(1024)S(1)} %pad_clamp_fusion.2), kind=kCustom, calls=%fused_computation.clone | custom fusion | bytes 525312 | tf_op jit(solution)/shard_map/jit(_take)/gather | solution.py:35
  40.1 2.4 %gather_fusion.3 = f32[256,256]{1,0:T(8,128)S(1)} fusion(f32[256,1536]{0,1:T(8,128)} %collective-permute-done, s32[1024]{0:T(1024)S(1)} %pad_clamp_fusion.1), kind=kCustom, calls=%fused_computation.1.clone | custom fusion | bytes 525312 | tf_op jit(solution)/shard_map/jit(_take)/gather | solution.py:39
  42.8 11.7 %cholesky.50 = f32[128,128]{1,0:T(8,128)S(1)} custom-call(f32[128,128]{1,0:T(8,128)S(1)} %cholesky.118), custom_call_target="Cholesky" | custom-call | tf_op jit(solution)/shard_map/jit(cholesky)/cholesky | solution.py:40
  54.5 0.7 compare_reduce_fusion.1
  55.2 9.8 %custom-call.18 = f32[1,128,128]{1,2,0:T(8,128)S(1)} custom-call(f32[1,128,128]{2,1,0:T(8,128)S(1)} %get-tuple-element.35), custom_call_target="InvertDiagBlocksLowerTriangular" | custom-call | tf_op jit(solution)/shard_map/jit(cholesky)/cholesky | solution.py:40
  65.5 11.7 %cholesky.105 = f32[128,128]{1,0:T(8,128)S(1)} custom-call(f32[128,128]{1,0:T(8,128)S(1)} %convolution_subtract_fusion.2), custom_call_target="Cholesky" | custom-call | tf_op jit(solution)/shard_map/jit(cholesky)/cholesky | solution.py:40
  77.3 0.7 compare_reduce_fusion
  79.4 4.2 %while.1 = (s32[]{:T(128)}, f32[256,256]{1,0:T(8,128)S(1)}, s32[2,2]{1,0:T(2,128)S(1)}, f32[2,128,128]{2,1,0:T(8,128)S(1)}, s32[]{:T(128)}) while((s32[]{:T(128)}, f32[256,256]{1,0:T(8,128)S(1)}, s32[2,2]{1,0:T(2,128)S(1)}, f32[2,128,128]{2,1,0:T(8,128)S(1)}, s32[]{:T(128)}) %tuple.28), condition=%wide.while_cond, body=%wide.while_body.sunk | while | flops 2 | bytes 131189 | solution.py:43
  79.6 0.6 fusion.29
  80.2 1.4 %bitcast_dynamic-update-slice_fusion.2 = f32[2,128,128]{2,1,0:T(8,128)S(1)} fusion(f32[2,128,128]{2,1,0:T(8,128)S(1)} %get-tuple-element.77, s32[]{:T(128)S(6)} %copy.17, f32[256,256]{1,0:T(8,128)S(1)} %get-tuple-element.80, s32[]{:T(128)} %bitcast.55, s32[]{:T(128)} %bitcast.56), kind=kLoop, calls=%fused_computation.4.clone.1 | loop fusion | bytes 131084 | tf_op jit(solution)/shard_map/jit(_cho_solve)/triangular_solve
  81.6 0.6 fusion.29
  82.2 1.4 %bitcast_dynamic-update-slice_fusion.2 = f32[2,128,128]{2,1,0:T(8,128)S(1)} fusion(f32[2,128,128]{2,1,0:T(8,128)S(1)} %get-tuple-element.77, s32[]{:T(128)S(6)} %copy.17, f32[256,256]{1,0:T(8,128)S(1)} %get-tuple-element.80, s32[]{:T(128)} %bitcast.55, s32[]{:T(128)} %bitcast.56), kind=kLoop, calls=%fused_computation.4.clone.1 | loop fusion | bytes 131084 | tf_op jit(solution)/shard_map/jit(_cho_solve)/triangular_solve
  83.6 19.7 %custom-call.19 = f32[2,128,128]{1,2,0:T(8,128)S(1)} custom-call(f32[2,128,128]{2,1,0:T(8,128)S(1)} %get-tuple-element.13), custom_call_target="InvertDiagBlocksLowerTriangular" | custom-call | tf_op jit(solution)/shard_map/jit(_cho_solve)/triangular_solve | solution.py:43
  103.3 0.4 fusion.8
  104.0 0.4 fusion.15
  104.7 0.4 convolution_subtract_fusion
  105.4 1.8 %broadcast_select_fusion.3 = (f32[256,1536]{0,1:T(8,128)S(1)}, f32[256,1536]{0,1:T(8,128)S(1)}) fusion(f32[256,1536]{0,1:T(8,128)S(1)} %copy-done.1, f32[256,1536]{0,1:T(8,128)} %collective-permute-done, pred[]{:T(512)S(6)} %eq.3), kind=kLoop, calls=%fused_computation.17 | loop fusion | flops 786432 | bytes 6291457 | tf_op jit(solution)/shard_map/jit(_where)/select_n | solution.py:41
  107.2 0.3 copy-done.2
  107.5 0.7 copy-done.3
  108.3 9.9 %fusion = f32[1,384,3072]{2,1,0:T(8,128)} fusion(f32[384,1536]{1,0:T(8,128)S(1)} %copy-done.3, f32[384,1536]{1,0:T(8,128)S(1)} %copy-done.2, f32[256,1536]{0,1:T(8,128)S(1)} %get-tuple-element.29, f32[256,1536]{0,1:T(8,128)S(1)} %get-tuple-element.28, f32[128,384]{1,0:T(8,128)S(1)} %fusion.14, f32[128,384]{1,0:T(8,128)S(1)} %fusion.13), kind=kOutput, calls=%fused_computation.7 | convolution fusion | flops 3627122688 | bytes 12976128 | tf_op jit(solution)/shard_map/dot_general | solution.py:44
  (35 shorter events, 2.2 us)
Async XLA Ops:
  3.5 6.4 %copy-start = (f32[1,384,1536]{2,1,0:T(8,128)S(1)}, f32[1,384,1536]{2,1,0:T(8,128)}, u32[]{:S(2)}) copy-start(f32[1,384,1536]{2,1,0:T(8,128)} %param.4) | copy-start | bytes 7077892
  4.8 23.5 %all-to-all-start = ((f32[4,64,1536]{2,1,0:T(8,128)}), f32[4,64,1536]{2,1,0:T(8,128)}, u32[]{:S(2)}, u32[]{:S(2)}) async-start(f32[4,64,1536]{2,1,0:T(8,128)} %stack.2), calls=%async_computation | async-start | bytes 3145728 | tf_op jit(solution)/shard_map/all_to_all | solution.py:33
  31.3 8.8 %collective-permute-start = (f32[256,1536]{0,1:T(8,128)}, f32[256,1536]{0,1:T(8,128)}, u32[]{:S(2)}, u32[]{:S(2)}) collective-permute-start(f32[256,1536]{0,1:T(8,128)} %copy.6), channel_id=1, source_target_pairs={{0,4},{4,0},{8,12},{12,8},{16,20},{20,16},{24,28},{28,24},{32,36},... | collective-permute-start | bytes 4718600 | tf_op jit(solution)/shard_map/ppermute | solution.py:14
  65.5 39.9 %copy-start.1 = (f32[256,1536]{0,1:T(8,128)S(1)}, f32[256,1536]{0,1:T(8,128)}, u32[]{:S(2)}) copy-start(f32[256,1536]{0,1:T(8,128)} %copy.6) | copy-start | bytes 4718596
  105.4 2.1 %copy-start.2 = (f32[384,1536]{1,0:T(8,128)S(1)}, f32[384,1536]{1,0:T(8,128)}, u32[]{:S(2)}) copy-start(f32[384,1536]{1,0:T(8,128)} %get-tuple-element.30) | copy-start | bytes 7077892
  105.4 2.8 %copy-start.3 = (f32[384,1536]{1,0:T(8,128)S(1)}, f32[384,1536]{1,0:T(8,128)}, u32[]{:S(2)}) copy-start(f32[384,1536]{1,0:T(8,128)} %get-tuple-element.31) | copy-start | bytes 7077892
